TPU v7x, 32 devices: a whole 2x2x4 slice. The times are simulated.
32 devices in a mesh: section: 2 (over core), ep: 4 (over z), tp: 4 (over y, x).
Axes of the slice: x: 2, y: 2, z: 4, core: 2. Of those that a mesh axis runs over, the one named last changes fastest.
Arguments:
- hidden: bfloat16 [512, 6144], P('ep', ('section', 'tp')), may hold values from -6 to 6
- expert_ids: int32 [512, 2], P('ep'), may hold values from 0 to 7, all different within a row; in each aligned block of 128 rows (0 to 127, 128 to 255, ...) at most 40 rows name the same one
- gate_weights: float32 [512, 2], P('ep'), may hold values from 0 to 1, as said below
- gate_proj: bfloat16 [4, 6144, 16384], P('ep', None, ('section', 'tp')), may hold values from -0.078125 to 0.078125
- up_proj: bfloat16 [4, 6144, 16384], P('ep', None, ('section', 'tp')), may hold values from -0.078125 to 0.078125
- down_proj: bfloat16 [4, 6144, 16384], P('ep', ('section', 'tp')), may hold values from -0.0625 to 0.0625
Outputs:
- moe_out: bfloat16 [512, 6144], P('ep', ('section', 'tp'))
Inputs may be any that keep to these rules, and one draw needn't show every extreme that they name: `expert_ids`: the two entries of a row differ. Within the 128 rows of one device no expert is named by more than 40 rows, and in some device's rows one expert is named by exactly 40. Every expert is named somewhere. `gate_weights`: the two weights of a token are positive, sum to one, and the first is at least the second.
All inputs are finite; a program needn't handle non-finite values.
Results may differ from a plain program's by a relative error of at most 0.0059.
Values may be sent and summed in bfloat16 or wider, within the bound.
A program may use at most 192 MiB of HBM per device.

v0:
```python
import jax
import jax.numpy as jnp
from jax import lax
from jax.sharding import PartitionSpec as P

E = 8
F = 8192
CAP = 40


def slot_tables(expert_ids, capacity, experts):
    token_count = expert_ids.shape[0]
    flat_ids = expert_ids.reshape(-1)
    onehot = (flat_ids[:, None] == jnp.arange(experts, dtype=jnp.int32)[None, :]).astype(jnp.int32)
    before = jnp.cumsum(onehot, axis=0) - onehot
    position = jnp.sum(before * onehot, axis=1)
    slot_of = (flat_ids * capacity + position).reshape(token_count, -1)
    slot_range = jnp.arange(experts * capacity, dtype=jnp.int32)
    matches_st = slot_of[None, :, :] == slot_range[:, None, None]
    dispatch = jnp.any(matches_st, axis=2).astype(jnp.bfloat16)
    return (dispatch, slot_of)


def on_device(hidden, expert_ids, gate_weights, gate_proj, up_proj, down_proj):
    ep_count = lax.axis_size("ep")
    share_count = lax.axis_size("section") * lax.axis_size("tp")
    owners_each = max(1, ep_count // E)
    experts_each = max(1, E // ep_count)
    local_cols = gate_proj.shape[2]
    group_cols = local_cols * share_count
    owner_index = lax.axis_index("ep")
    share_index = lax.axis_index("section") * lax.axis_size("tp") + lax.axis_index("tp")
    own_expert = (owner_index * group_cols + share_index * local_cols) // F
    slot_expert = owner_index // owners_each * experts_each + jnp.arange(
        experts_each, dtype=jnp.int32
    )
    keep_mask = (slot_expert == own_expert).reshape(1, experts_each, 1, 1)
    gate_local = gate_proj[0]
    up_local = up_proj[0]
    down_local = down_proj[0]
    dispatch, slot_of = slot_tables(expert_ids, CAP, E)
    packed = jnp.dot(
        dispatch,
        lax.all_gather(hidden, ("section", "tp"), axis=1, tiled=True),
        preferred_element_type=jnp.float32,
    ).astype(jnp.bfloat16)
    grouped = packed.reshape(E // experts_each, experts_each, CAP, packed.shape[1])
    received = lax.all_to_all(
        jnp.repeat(grouped, owners_each, axis=0), "ep", split_axis=0, concat_axis=0, tiled=True
    )
    flat_rows = received.reshape(-1, received.shape[3])
    gate_out = jnp.dot(flat_rows, gate_local, preferred_element_type=jnp.float32)
    up_out = jnp.dot(flat_rows, up_local, preferred_element_type=jnp.float32)
    lead_shape = received.shape[:3]
    activated = (jax.nn.silu(gate_out) * up_out).reshape(lead_shape + (local_cols,))
    activated = jnp.where(keep_mask, activated, 0.0).astype(jnp.bfloat16)
    flat_act = activated.reshape(-1, local_cols)
    outputs = lax.dot_general(
        lax.all_gather(flat_act, ("section", "tp"), axis=1, tiled=True),
        down_local,
        (((1,), (1,)), ((), ())),
        preferred_element_type=jnp.float32,
    )
    outputs = outputs.reshape(lead_shape + (down_local.shape[0],)).astype(jnp.bfloat16)
    returned = lax.all_to_all(outputs, "ep", split_axis=0, concat_axis=0, tiled=True)
    grouped = returned.astype(jnp.float32).reshape(
        E // experts_each, owners_each, experts_each, CAP, returned.shape[3]
    )
    summed = jnp.sum(grouped, axis=1).reshape(E * CAP, returned.shape[3])
    first_rows = summed[slot_of[:, 0]]
    second_rows = summed[slot_of[:, 1]]
    combined_out = gate_weights[:, 0:1] * first_rows + gate_weights[:, 1:2] * second_rows
    return combined_out.astype(jnp.bfloat16)


def on_device_paired(hidden, expert_ids, gate_weights, gate_proj, up_proj, down_proj):
    ep_count = lax.axis_size("ep")
    pair = lax.axis_size("section")
    width = hidden.shape[1]
    local_cols = gate_proj.shape[2]
    dispatch, slot_of = slot_tables(expert_ids, CAP, E)
    packed = jnp.dot(dispatch, hidden, preferred_element_type=jnp.float32).astype(jnp.bfloat16)
    sent = packed.reshape(ep_count, pair, CAP, width)
    received = lax.all_to_all(sent, "ep", split_axis=0, concat_axis=0, tiled=True)
    swapped = lax.all_to_all(received, "section", split_axis=1, concat_axis=1, tiled=True)
    halves = lax.all_gather(swapped, "tp", axis=0)
    rows = jnp.transpose(halves, (1, 3, 2, 0, 4)).reshape(ep_count * CAP, -1)
    gate_out = jnp.dot(rows, gate_proj[0], preferred_element_type=jnp.float32)
    up_out = jnp.dot(rows, up_proj[0], preferred_element_type=jnp.float32)
    activated = (jax.nn.silu(gate_out) * up_out).astype(jnp.bfloat16)
    gathered = lax.all_gather(activated, "tp", axis=1, tiled=True)
    both = lax.all_gather(gathered, "section", axis=0)
    outputs = jnp.stack(
        [
            lax.dot_general(
                both[i],
                down_proj[0][:, i * F : (i + 1) * F],
                (((1,), (1,)), ((), ())),
                preferred_element_type=jnp.float32,
            )
            .astype(jnp.bfloat16)
            .reshape(ep_count, CAP, width)
            for i in range(pair)
        ],
        axis=1,
    )
    returned = lax.all_to_all(outputs, "ep", split_axis=0, concat_axis=0, tiled=True)
    flat = returned.reshape(E * CAP, width)
    slot_range = jnp.arange(E * CAP, dtype=jnp.int32)[None, :]
    picks = [(slot_of[:, k : k + 1] == slot_range).astype(jnp.bfloat16) for k in range(2)]
    first_rows, second_rows = [jnp.dot(p, flat, preferred_element_type=jnp.float32) for p in picks]
    combined = gate_weights[:, 0:1] * first_rows + gate_weights[:, 1:2] * second_rows
    return combined.astype(jnp.bfloat16)


def solution(mesh):

    def body(*args):
        paired = (
            E // mesh.shape["ep"] == mesh.shape["section"]
            and args[3].shape[2] * mesh.shape["tp"] == F
        )
        return (on_device_paired if paired else on_device)(*args)

    return jax.shard_map(
        body,
        mesh=mesh,
        in_specs=(
            P("ep", ("section", "tp")),
            P("ep", None),
            P("ep", None),
            P("ep", None, ("section", "tp")),
            P("ep", None, ("section", "tp")),
            P("ep", ("section", "tp"), None),
        ),
        out_specs=P("ep", ("section", "tp")),
        check_vma=False,
    )
```

profile of v0, /device:TPU:0, one launch (start us, length us, event | category | flops | bytes accessed | tf_op | source)
XLA Modules:
  0.0 201.5 jit_solution(15060545460979945678)
XLA Ops:
  6.5 0.0 copy-start
  6.5 0.0 all-gather.8.cloned.1.call-start
  6.5 0.8 copy.49
  7.4 0.1 eq.72
  7.5 0.1 eq.68
  7.7 0.6 reduce-window.6
  8.2 0.2 slice_reduce_fusion
  8.5 0.1 fusion.32
  8.6 0.1 reduce_sum.12
  8.7 0.1 copy.51
  8.8 0.7 multiply_add_fusion
  9.6 0.0 copy-done
  9.6 0.3 convolution_convert_fusion
  9.8 19.9 %all_to_all.15 = bf16[4,2,40,768]{3,2,1,0:T(8,128)(2,1)S(1)} all-to-all(bf16[4,2,40,768]{3,2,1,0:T(8,128)(2,1)S(1)} %bitcast.47), channel_id=1, replica_groups=mesh['section'=2,'ep'=4,'tp'=4] {'ep'}, dimensions={0} | all-to-all | bytes 983040 | tf_op jit(solution)/shard_map/all_to_all | solution.py:84
  29.8 4.1 %all_to_all.16 = bf16[4,2,40,768]{3,2,0,1:T(8,128)(2,1)S(1)} all-to-all(bf16[4,2,40,768]{3,2,0,1:T(8,128)(2,1)S(1)} %copy.52), channel_id=1, replica_groups=mesh['section'=2,'ep'=4,'tp'=4] {'section'}, dimensions={1} | all-to-all | bytes 983040 | tf_op jit(solution)/shard_map/all_to_all | solution.py:85
  33.9 0.8 copy.53
  34.7 0.0 all-gather.8.cloned.1.call-update
  34.7 0.0 all-gather.6.cloned.1.call-start
  34.8 33.4 %all-gather.8.cloned.1.call-done = bf16[16,2,40,768]{3,2,1,0:T(8,128)(2,1)} async-done(((bf16[4,2,40,768]{3,2,1,0:T(8,128)(2,1)}), bf16[16,2,40,768]{3,2,1,0:T(8,128)(2,1)}) %all-gather.8.cloned.1.call-update) | async-done | bytes 1966096 | tf_op jit(solution)/shard_map/all_gather | solution.py:86
  68.2 3.1 %copy.54 = bf16[4,40,2,4,768]{4,3,2,1,0:T(4,128)(2,1)S(1)} copy(bf16[4,40,2,4,768]{4,1,2,0,3:T(8,128)(2,1)} %bitcast.46) | data formatting | bytes 3932160 | tf_op jit(solution)/shard_map/transpose | solution.py:87
  71.3 2.4 %reshape.37 = bf16[160,6144]{1,0:T(8,128)(2,1)} reshape(bf16[4,40,2,4,768]{4,3,2,1,0:T(4,128)(2,1)S(1)} %copy.54) | data formatting | bytes 3932160 | tf_op jit(solution)/shard_map/reshape | solution.py:87
  73.8 0.0 copy-start.2
  73.8 12.9 %fusion.2 = f32[160,2048]{1,0:T(8,128)S(1)} fusion(bf16[160,6144]{1,0:T(8,128)(2,1)} %reshape.37, bf16[1,6144,2048]{2,1,0:T(8,128)(2,1)} %param.9), kind=kOutput, calls=%fused_computation.2 | convolution fusion | flops 4026531840 | bytes 28442624 | tf_op jit(solution)/shard_map/dot_general | solution.py:88
  86.7 0.0 copy-done.2
  86.7 11.6 %fusion.13 = bf16[160,2048]{1,0:T(8,128)(2,1)} fusion(bf16[160,6144]{1,0:T(8,128)(2,1)S(1)} %copy-done.2, bf16[1,6144,2048]{2,1,0:T(8,128)(2,1)} %param.10, f32[160,2048]{1,0:T(8,128)S(1)} %fusion.2), kind=kOutput, calls=%fused_computation.11 | convolution fusion | flops 4028497920 | bytes 29097984 | tf_op jit(solution)/shard_map/dot_general | solution.py:89
  98.3 0.0 all-gather.6.cloned.1.call-update
  98.3 0.2 all-gather.10.cloned.1.call-start
  98.5 39.6 %all-gather.6.cloned.1.call-done = bf16[160,8192]{1,0:T(8,128)(2,1)} async-done(((bf16[160,2048]{1,0:T(8,128)(2,1)}), bf16[160,8192]{1,0:T(8,128)(2,1)}) %all-gather.6.cloned.1.call-update) | async-done | bytes 2621456 | tf_op jit(solution)/shard_map/all_gather | solution.py:91
  138.1 0.0 all-gather.10.cloned.1.call-update
  138.1 16.8 %all-gather.10.cloned.1.call-done = bf16[320,8192]{1,0:T(8,128)(2,1)} async-done(((bf16[160,8192]{1,0:T(8,128)(2,1)}), bf16[320,8192]{1,0:T(8,128)(2,1)}) %all-gather.10.cloned.1.call-update) | async-done | bytes 5242896 | tf_op jit(solution)/shard_map/all_gather | solution.py:92
  154.9 0.0 copy-start.4
  154.9 9.8 %fusion.17 = bf16[160,768]{1,0:T(8,128)(2,1)S(1)} fusion(bf16[768,16384]{1,0:T(8,128)(2,1)} %bitcast.50, bf16[320,8192]{1,0:T(8,128)(2,1)} %all-gather.10.cloned.1.call-done), kind=kOutput, calls=%fused_computation.16 | convolution fusion | flops 2013388800 | bytes 15450112 | tf_op jit(solution)/shard_map/dot_general | solution.py:95
  164.7 0.0 copy-done.4
  164.7 0.0 copy-start.3
  164.7 0.0 copy-start.1
  164.7 8.9 %fusion.22 = bf16[160,768]{1,0:T(8,128)(2,1)S(1)} fusion(bf16[768,16384]{1,0:T(8,128)(2,1)} %bitcast.51, bf16[320,8192]{1,0:T(8,128)(2,1)S(1)} %copy-done.4), kind=kOutput, calls=%fused_computation.17 | convolution fusion | flops 2013388800 | bytes 15450112 | tf_op jit(solution)/shard_map/dot_general | solution.py:95
  173.7 0.8 pad_maximum_fusion
  174.5 4.9 %all-to-all-start.2 = ((bf16[4,2,40,768]{3,2,1,0:T(8,128)(2,1)}), bf16[4,2,40,768]{3,2,1,0:T(8,128)(2,1)S(1)}, u32[]{:S(2)}, u32[]{:S(2)}) async-start(bf16[4,2,40,768]{3,2,1,0:T(8,128)(2,1)} %pad_maximum_fusion), calls=%async_computation.2 | async-start | bytes 983040 | tf_op jit(solution)/shard_map/all_to_all | solution.py:107
  179.4 0.0 copy-done.3
  179.4 14.2 %all-to-all-done.2 = bf16[4,2,40,768]{3,2,1,0:T(8,128)(2,1)S(1)} async-done(((bf16[4,2,40,768]{3,2,1,0:T(8,128)(2,1)}), bf16[4,2,40,768]{3,2,1,0:T(8,128)(2,1)S(1)}, u32[]{:S(2)}, u32[]{:S(2)}) %all-to-all-start.2) | async-done | bytes 491552 | tf_op jit(solution)/shard_map/all_to_all | solution.py:107
  193.6 0.3 convolution_multiply_fusion
  193.9 1.0 fusion.27
  194.9 0.0 copy-done.1
  (7 shorter events, 0.1 us)
Async XLA Ops:
  6.5 3.0 %copy-start = (bf16[128,768]{1,0:T(8,128)(2,1)S(1)}, bf16[128,768]{1,0:T(8,128)(2,1)}, u32[]{:S(2)}) copy-start(bf16[128,768]{1,0:T(8,128)(2,1)} %param.6) | copy-start | bytes 589828
  6.5 61.7 %all-gather.8.cloned.1.call-start = ((), (), s32[]{:S(2)}) async-start(), calls=%async_computation.4 | async-start | bytes 2457600 | tf_op jit(solution)/shard_map/all_gather | solution.py:86
  34.7 103.4 %all-gather.6.cloned.1.call-start = ((), (), s32[]{:S(2)}) async-start(), calls=%async_computation.3 | async-start | bytes 3276800 | tf_op jit(solution)/shard_map/all_gather | solution.py:91
  73.8 12.9 %copy-start.2 = (bf16[160,6144]{1,0:T(8,128)(2,1)S(1)}, bf16[160,6144]{1,0:T(8,128)(2,1)}, u32[]{:S(2)}) copy-start(bf16[160,6144]{1,0:T(8,128)(2,1)} %reshape.37) | copy-start | bytes 5898244
  98.3 56.6 %all-gather.10.cloned.1.call-start = ((), (), s32[]{:S(2)}) async-start(), calls=%async_computation.5 | async-start | bytes 7864320 | tf_op jit(solution)/shard_map/all_gather | solution.py:92
  154.9 9.8 %copy-start.4 = (bf16[320,8192]{1,0:T(8,128)(2,1)S(1)}, bf16[320,8192]{1,0:T(8,128)(2,1)}, u32[]{:S(2)}) copy-start(bf16[320,8192]{1,0:T(8,128)(2,1)} %all-gather.10.cloned.1.call-done) | copy-start | bytes 15728644
  164.7 14.7 %copy-start.3 = (f32[128,2]{0,1:T(2,128)S(1)}, f32[128,2]{0,1:T(2,128)}, u32[]{:S(2)}) copy-start(f32[128,2]{0,1:T(2,128)} %param.8) | copy-start | bytes 3076
  164.7 30.2 %copy-start.1 = (bf16[128,768]{1,0:T(8,128)(2,1)S(1)}, bf16[128,768]{1,0:T(8,128)(2,1)}, u32[]{:S(2)}) copy-start(bf16[128,768]{1,0:T(8,128)(2,1)} %param.6) | copy-start | bytes 589828
  174.5 19.1 %all-to-all-start.2 = ((bf16[4,2,40,768]{3,2,1,0:T(8,128)(2,1)}), bf16[4,2,40,768]{3,2,1,0:T(8,128)(2,1)S(1)}, u32[]{:S(2)}, u32[]{:S(2)}) async-start(bf16[4,2,40,768]{3,2,1,0:T(8,128)(2,1)} %pad_maximum_fusion), calls=%async_computation.2 | async-start | bytes 983040 | tf_op jit(solution)/shard_map/all_to_all | solution.py:107
Sparse Core Ops, SparseCore 0:
  34.9 33.3 all-gather.7
  98.4 39.6 all-gather.5
  139.7 15.2 all-gather.9
where the time goes:
time: 202 us; the launch traced here: 201 us
  waiting for transfers between devices  104 us (51%)
  matrix products  44.8 us (22%)
  blocking collectives  24 us (12%)
  between operations  13.2 us (7%)
  local copies, waits for them, and re-layouts  7.91 us (4%)
  starting transfers between devices  5.12 us (3%)
  other arithmetic  2.28 us (1%)
    all_gather x1, waiting for transfers between devices, on_device_paired(): gathered = lax.all_gather(activated, 'tp', axis=1, tiled=True)  39.6 us
    all_gather x1, waiting for transfers between devices, on_device_paired(): halves = lax.all_gather(swapped, 'tp', axis=0)  33.4 us
    all_to_all x1, blocking collectives, on_device_paired(): lax.all_to_all(sent, 'ep', split_axis=0, concat_axis=0, tiled=True)  19.9 us
    dot_general x2, matrix products, on_device_paired(): lax.dot_general(both[i], down_proj[0][:, i * F:(i + 1) * F], (((1,), (1,)...  18.7 us
    all_gather x1, waiting for transfers between devices, on_device_paired(): both = lax.all_gather(gathered, 'section', axis=0)  16.8 us
    all_to_all x1, waiting for transfers between devices, on_device_paired(): lax.all_to_all(outputs, 'ep', split_axis=0, concat_axis=0, tiled=True)  14.2 us
    dot_general x1, matrix products, on_device_paired(): gate_out = jnp.dot(rows, gate_proj[0], preferred_element_type=jnp.float32)  12.9 us
    dot_general x1, matrix products, on_device_paired(): up_out = jnp.dot(rows, up_proj[0], preferred_element_type=jnp.float32)  11.6 us
  transfers between devices with their start and end apart: 4, of which 4 were waited for; matrix products, arithmetic and copies ran while one was open for 0% of the time, Pallas kernels for 0%

commit v1 on v0

--- a/solution.py
+++ b/solution.py
@@ -6,6 +6,12 @@
 E = 8
 F = 8192
 CAP = 40
+
+
+def change_spot(content, axis_no):
+    value_now = list(content.shape[1:])
+    value_now[axis_no] *= content.shape[0]
+    return jnp.moveaxis(content, 0, axis_no).reshape(value_now)
 
 
 def slot_tables(expert_ids, capacity, experts):
@@ -74,6 +80,22 @@
 
 
 def on_device_paired(hidden, expert_ids, gate_weights, gate_proj, up_proj, down_proj):
+
+    def _connect_desk(arr_in, dev_axis, row_dim):
+        n_all = jax.lax.axis_size(dev_axis)
+        cards = [(h, (h + 1) % n_all) for h in range(n_all)]
+        shelf = [(src_i, w) for w, src_i in cards]
+        moved, d_next = ([], [])
+        for i0 in range(n_all - 1):
+            if i0 % 2 == 0:
+                moved.append(jax.lax.ppermute(moved[-1] if moved else arr_in, dev_axis, cards))
+            else:
+                d_next.append(jax.lax.ppermute(d_next[-1] if d_next else arr_in, dev_axis, shelf))
+        w2 = jnp.stack([*moved[::-1], arr_in, *d_next], axis=0)
+        parts_out = jax.lax.axis_index(dev_axis) - len(moved)
+        w2 = w2[(jnp.arange(n_all) - parts_out) % n_all]
+        return change_spot(w2, row_dim)
+
     ep_count = lax.axis_size("ep")
     pair = lax.axis_size("section")
     width = hidden.shape[1]
@@ -88,7 +110,7 @@
     gate_out = jnp.dot(rows, gate_proj[0], preferred_element_type=jnp.float32)
     up_out = jnp.dot(rows, up_proj[0], preferred_element_type=jnp.float32)
     activated = (jax.nn.silu(gate_out) * up_out).astype(jnp.bfloat16)
-    gathered = lax.all_gather(activated, "tp", axis=1, tiled=True)
+    gathered = _connect_desk(activated, "tp", 1)
     both = lax.all_gather(gathered, "section", axis=0)
     outputs = jnp.stack(
         [

time: 202 us -> 218 us (1.079)
  local copies, waits for them, and re-layouts: 7.91 us -> 18.4 us
  starting transfers between devices: 5.12 us -> 8.44 us
    ppermute x0 -> x3, waiting for transfers between devices: none -> 41.9 us  [the longest x2 28.5 us: _connect_desk(): jax.lax.ppermute(moved[-1] if moved else arr_in, dev_axis, cards)]
    all_gather x1 -> x0, waiting for transfers between devices: 39.6 us -> none  [on_device_paired(): gathered = lax.all_gather(activated, 'tp', axis=1, tiled=True)]
    transpose x0 -> x1, local copies, waits for them, and re-layouts: none -> 3.76 us  [change_spot(): return jnp.moveaxis(content, 0, axis_no).reshape(value_now)]
    another operation x1 -> x2, local copies, waits for them, and re-layouts: 0.01 us -> 3.59 us  [the longest x1 3.59 us: on_device_paired(): both = lax.all_gather(gathered, 'section', axis=0)]
    ppermute x0 -> x3, starting transfers between devices: none -> 3.54 us  [the longest x2 2.08 us: _connect_desk(): jax.lax.ppermute(moved[-1] if moved else arr_in, dev_axis, cards)]
    gather x0 -> x1, local copies, waits for them, and re-layouts: none -> 2.24 us  [_connect_desk(): w2 = w2[(jnp.arange(n_all) - parts_out) % n_all]]
  transfers between devices with their start and end apart: 4 -> 6, of which waited for: 4 -> 6; matrix products, arithmetic and copies ran while one was open for 0% -> 0% of each run, Pallas kernels for 0% -> 0%
where the time goes in v1:
time: 218 us; the launch traced here: 217 us
  waiting for transfers between devices  105 us (48%)
  matrix products  44 us (20%)
  blocking collectives  24 us (11%)
  local copies, waits for them, and re-layouts  18.4 us (8%)
  between operations  13.5 us (6%)
  starting transfers between devices  8.44 us (4%)
  other arithmetic  4.12 us (2%)
    all_gather x1, waiting for transfers between devices, on_device_paired(): halves = lax.all_gather(swapped, 'tp', axis=0)  33.4 us
    ppermute x2, waiting for transfers between devices, _connect_desk(): jax.lax.ppermute(moved[-1] if moved else arr_in, dev_axis, cards)  28.5 us
    all_to_all x1, blocking collectives, on_device_paired(): lax.all_to_all(sent, 'ep', split_axis=0, concat_axis=0, tiled=True)  19.9 us
    dot_general x2, matrix products, on_device_paired(): lax.dot_general(both[i], down_proj[0][:, i * F:(i + 1) * F], (((1,), (1,)...  18.7 us
    all_gather x1, waiting for transfers between devices, on_device_paired(): both = lax.all_gather(gathered, 'section', axis=0)  15.4 us
    all_to_all x1, waiting for transfers between devices, on_device_paired(): lax.all_to_all(outputs, 'ep', split_axis=0, concat_axis=0, tiled=True)  14.2 us
    ppermute x1, waiting for transfers between devices, _connect_desk(): jax.lax.ppermute(d_next[-1] if d_next else arr_in, dev_axis, shelf)  13.5 us
    dot_general x1, matrix products, on_device_paired(): gate_out = jnp.dot(rows, gate_proj[0], preferred_element_type=jnp.float32)  12.9 us
  transfers between devices with their start and end apart: 6, of which 6 were waited for; matrix products, arithmetic and copies ran while one was open for 0% of the time, Pallas kernels for 0%

profile of v1, /device:TPU:0, one launch (start us, length us, event | category | flops | bytes accessed | tf_op | source)
XLA Modules:
  0.0 217.5 jit_solution(8398614679854551324)
XLA Ops:
  6.5 0.0 copy-start
  6.5 0.0 all-gather.6.cloned.1.call-start
  6.5 0.8 copy.54
  7.4 0.1 eq.74
  7.5 0.1 eq.70
  7.7 0.6 reduce-window.6
  8.2 0.2 slice_reduce_fusion
  8.5 0.1 fusion.26
  8.6 0.1 reduce_sum.12
  8.7 0.1 copy.56
  8.8 0.7 multiply_add_fusion
  9.6 0.0 copy-done
  9.6 0.3 convolution_convert_fusion
  9.8 19.9 %all_to_all.15 = bf16[4,2,40,768]{3,2,1,0:T(8,128)(2,1)S(1)} all-to-all(bf16[4,2,40,768]{3,2,1,0:T(8,128)(2,1)S(1)} %bitcast.65), channel_id=1, replica_groups=mesh['section'=2,'ep'=4,'tp'=4] {'ep'}, dimensions={0} | all-to-all | bytes 983040 | tf_op jit(solution)/shard_map/all_to_all | solution.py:106
  29.8 4.1 %all_to_all.16 = bf16[4,2,40,768]{3,2,0,1:T(8,128)(2,1)S(1)} all-to-all(bf16[4,2,40,768]{3,2,0,1:T(8,128)(2,1)S(1)} %copy.57), channel_id=1, replica_groups=mesh['section'=2,'ep'=4,'tp'=4] {'section'}, dimensions={1} | all-to-all | bytes 983040 | tf_op jit(solution)/shard_map/all_to_all | solution.py:107
  33.9 0.8 copy.58
  34.7 0.0 all-gather.6.cloned.1.call-update
  34.7 0.0 all-gather.4.cloned.1.call-start
  34.8 33.4 %all-gather.6.cloned.1.call-done = bf16[16,2,40,768]{3,2,1,0:T(8,128)(2,1)} async-done(((bf16[4,2,40,768]{3,2,1,0:T(8,128)(2,1)}), bf16[16,2,40,768]{3,2,1,0:T(8,128)(2,1)}) %all-gather.6.cloned.1.call-update) | async-done | bytes 1966096 | tf_op jit(solution)/shard_map/all_gather | solution.py:108
  68.2 3.1 %copy.59 = bf16[4,40,2,4,768]{4,3,2,1,0:T(4,128)(2,1)S(1)} copy(bf16[4,40,2,4,768]{4,1,2,0,3:T(8,128)(2,1)} %bitcast.64) | data formatting | bytes 3932160 | tf_op jit(solution)/shard_map/transpose | solution.py:109
  71.3 2.5 %reshape.86 = bf16[160,6144]{1,0:T(8,128)(2,1)} reshape(bf16[4,40,2,4,768]{4,3,2,1,0:T(4,128)(2,1)S(1)} %copy.59) | data formatting | bytes 3932160 | tf_op jit(solution)/shard_map/reshape | solution.py:109
  73.8 0.0 copy-start.2
  73.8 12.9 %fusion.2 = f32[160,2048]{1,0:T(8,128)S(1)} fusion(bf16[160,6144]{1,0:T(8,128)(2,1)} %reshape.86, bf16[1,6144,2048]{2,1,0:T(8,128)(2,1)} %param.9), kind=kOutput, calls=%fused_computation.3 | convolution fusion | flops 4026531840 | bytes 28442624 | tf_op jit(solution)/shard_map/dot_general | solution.py:110
  86.7 0.0 copy-done.2
  86.7 10.8 %fusion.11 = bf16[160,2048]{1,0:T(8,128)(2,1)S(1)} fusion(bf16[160,6144]{1,0:T(8,128)(2,1)S(1)} %copy-done.2, bf16[1,6144,2048]{2,1,0:T(8,128)(2,1)} %param.10, f32[160,2048]{1,0:T(8,128)S(1)} %fusion.2), kind=kOutput, calls=%fused_computation.13 | convolution fusion | flops 4028497920 | bytes 29097984 | tf_op jit(solution)/shard_map/dot_general | solution.py:111
  97.5 1.5 collective-permute-start
  99.0 1.5 collective-permute-start.2
  100.4 15.6 %collective-permute-done = bf16[160,2048]{1,0:T(8,128)(2,1)S(1)} collective-permute-done((bf16[160,2048]{1,0:T(8,128)(2,1)S(1)}, bf16[160,2048]{1,0:T(8,128)(2,1)S(1)}, u32[]{:S(2)}, u32[]{:S(2)}) %collective-permute-start) | collective-permute-done | bytes 655392 | tf_op jit(solution)/shard_map/ppermute | solution.py:91
  116.0 0.0 copy-start.3
  116.0 0.6 collective-permute-start.1
  116.6 13.5 %collective-permute-done.2 = bf16[160,2048]{1,0:T(8,128)(2,1)S(1)} collective-permute-done((bf16[160,2048]{1,0:T(8,128)(2,1)S(1)}, bf16[160,2048]{1,0:T(8,128)(2,1)S(1)}, u32[]{:S(2)}, u32[]{:S(2)}) %collective-permute-start.2) | collective-permute-done | bytes 655392 | tf_op jit(solution)/shard_map/ppermute | solution.py:93
  130.1 0.0 copy-start.4
  130.1 12.9 %collective-permute-done.1 = bf16[160,2048]{1,0:T(8,128)(2,1)S(1)} collective-permute-done((bf16[160,2048]{1,0:T(8,128)(2,1)S(1)}, bf16[160,2048]{1,0:T(8,128)(2,1)S(1)}, u32[]{:S(2)}, u32[]{:S(2)}) %collective-permute-start.1) | collective-permute-done | bytes 655392 | tf_op jit(solution)/shard_map/ppermute | solution.py:91
  143.0 0.0 copy-start.5
  143.0 0.0 copy-done.3
  143.0 0.0 copy-done.4
  143.0 0.9 copy-done.5
  143.9 1.8 pad_maximum_fusion
  145.7 2.2 %gather_fusion = bf16[4,160,2048]{2,1,0:T(8,128)(2,1)} fusion(bf16[4,160,2048]{2,1,0:T(8,128)(2,1)S(1)} %pad_maximum_fusion, s32[1024]{0:T(1024)S(1)} %pad_clamp_fusion), kind=kCustom, calls=%fused_computation | custom fusion | bytes 5242896 | tf_op jit(solution)/shard_map/gather | solution.py:96
  147.9 3.8 %copy.60 = bf16[160,4,2048]{2,1,0:T(4,128)(2,1)S(1)} copy(bf16[160,4,2048]{2,0,1:T(8,128)(2,1)} %bitcast.61) | data formatting | bytes 5242880 | tf_op jit(solution)/shard_map/transpose | solution.py:14
  151.7 3.6 %all_gather_reshape.3 = bf16[1,160,8192]{2,1,0:T(8,128)(2,1)} reshape(bf16[160,4,2048]{2,1,0:T(4,128)(2,1)S(1)} %copy.60) | data formatting | bytes 5242880 | tf_op jit(solution)/shard_map/all_gather;reshape | solution.py:114
  155.3 0.0 all-gather.4.cloned.1.call-update
  155.3 15.4 %all-gather.4.cloned.1.call-done = bf16[2,160,8192]{2,1,0:T(8,128)(2,1)} async-done(((bf16[1,160,8192]{2,1,0:T(8,128)(2,1)}), bf16[2,160,8192]{2,1,0:T(8,128)(2,1)}) %all-gather.4.cloned.1.call-update) | async-done | bytes 5242896 | tf_op jit(solution)/shard_map/all_gather | solution.py:114
  170.7 0.0 copy-start.7
  170.7 9.8 %fusion.15 = bf16[160,768]{1,0:T(8,128)(2,1)S(1)} fusion(bf16[768,16384]{1,0:T(8,128)(2,1)} %bitcast.72, bf16[2,160,8192]{2,1,0:T(8,128)(2,1)} %all-gather.4.cloned.1.call-done), kind=kOutput, calls=%fused_computation.18 | convolution fusion | flops 2013388800 | bytes 15450112 | tf_op jit(solution)/shard_map/dot_general | solution.py:117
  180.5 0.0 copy-done.7
  180.5 0.0 copy-start.6
  180.5 0.0 copy-start.1
  180.5 8.9 %fusion.18 = bf16[160,768]{1,0:T(8,128)(2,1)S(1)} fusion(bf16[768,16384]{1,0:T(8,128)(2,1)} %bitcast.73, bf16[2,160,8192]{2,1,0:T(8,128)(2,1)S(1)} %copy-done.7), kind=kOutput, calls=%fused_computation.19 | convolution fusion | flops 2013388800 | bytes 15450112 | tf_op jit(solution)/shard_map/dot_general | solution.py:117
  189.4 0.8 pad_maximum_fusion.1
  190.2 4.9 %all-to-all-start.2 = ((bf16[4,2,40,768]{3,2,1,0:T(8,128)(2,1)}), bf16[4,2,40,768]{3,2,1,0:T(8,128)(2,1)S(1)}, u32[]{:S(2)}, u32[]{:S(2)}) async-start(bf16[4,2,40,768]{3,2,1,0:T(8,128)(2,1)} %pad_maximum_fusion.1), calls=%async_computation.2 | async-start | bytes 983040 | tf_op jit(solution)/shard_map/all_to_all | solution.py:129
  195.1 0.0 copy-done.6
  195.1 14.2 %all-to-all-done.2 = bf16[4,2,40,768]{3,2,1,0:T(8,128)(2,1)S(1)} async-done(((bf16[4,2,40,768]{3,2,1,0:T(8,128)(2,1)}), bf16[4,2,40,768]{3,2,1,0:T(8,128)(2,1)S(1)}, u32[]{:S(2)}, u32[]{:S(2)}) %all-to-all-start.2) | async-done | bytes 491552 | tf_op jit(solution)/shard_map/all_to_all | solution.py:129
  209.3 0.3 convolution_multiply_fusion
  209.7 1.0 fusion.21
  210.7 0.0 copy-done.1
  (9 shorter events, 0.1 us)
Async XLA Ops:
  6.5 3.0 %copy-start = (bf16[128,768]{1,0:T(8,128)(2,1)S(1)}, bf16[128,768]{1,0:T(8,128)(2,1)}, u32[]{:S(2)}) copy-start(bf16[128,768]{1,0:T(8,128)(2,1)} %param.6) | copy-start | bytes 589828
  6.5 61.7 %all-gather.6.cloned.1.call-start = ((), (), s32[]{:S(2)}) async-start(), calls=%async_computation.4 | async-start | bytes 2457600 | tf_op jit(solution)/shard_map/all_gather | solution.py:108
  34.7 135.9 %all-gather.4.cloned.1.call-start = ((), (), s32[]{:S(2)}) async-start(), calls=%async_computation.3 | async-start | bytes 7864320 | tf_op jit(solution)/shard_map/all_gather | solution.py:114
  73.8 12.9 %copy-start.2 = (bf16[160,6144]{1,0:T(8,128)(2,1)S(1)}, bf16[160,6144]{1,0:T(8,128)(2,1)}, u32[]{:S(2)}) copy-start(bf16[160,6144]{1,0:T(8,128)(2,1)} %reshape.86) | copy-start | bytes 5898244
  97.5 18.6 %collective-permute-start = (bf16[160,2048]{1,0:T(8,128)(2,1)S(1)}, bf16[160,2048]{1,0:T(8,128)(2,1)S(1)}, u32[]{:S(2)}, u32[]{:S(2)}) collective-permute-start(bf16[160,2048]{1,0:T(8,128)(2,1)S(1)} %fusion.11), channel_id=1, source_target_pairs={{0,1},{1,2},{2,3},{3,0},{4,5},{5,6},{6,7},{7,4},{8,9},{9,10},{10,1... | collective-permute-start | bytes 1966088 | tf_op jit(solution)/shard_map/ppermute | solution.py:91
  99.0 31.1 %collective-permute-start.2 = (bf16[160,2048]{1,0:T(8,128)(2,1)S(1)}, bf16[160,2048]{1,0:T(8,128)(2,1)S(1)}, u32[]{:S(2)}, u32[]{:S(2)}) collective-permute-start(bf16[160,2048]{1,0:T(8,128)(2,1)S(1)} %fusion.11), channel_id=1, source_target_pairs={{1,0},{2,1},{3,2},{0,3},{5,4},{6,5},{7,6},{4,7},{9,8},{10,9},{11,1... | collective-permute-start | bytes 1966088 | tf_op jit(solution)/shard_map/ppermute | solution.py:93
  116.0 26.9 %copy-start.3 = (bf16[160,2048]{1,0:T(8,128)(2,1)}, bf16[160,2048]{1,0:T(8,128)(2,1)S(1)}, u32[]{:S(2)}) copy-start(bf16[160,2048]{1,0:T(8,128)(2,1)S(1)} %collective-permute-done) | copy-start | bytes 1966084
  116.0 26.9 %collective-permute-start.1 = (bf16[160,2048]{1,0:T(8,128)(2,1)S(1)}, bf16[160,2048]{1,0:T(8,128)(2,1)S(1)}, u32[]{:S(2)}, u32[]{:S(2)}) collective-permute-start(bf16[160,2048]{1,0:T(8,128)(2,1)S(1)} %collective-permute-done), channel_id=1, source_target_pairs={{0,1},{1,2},{2,3},{3,0},{4,5},{5,6},{6,7},{7,4},{8,9},{9,10},{10,1... | collective-permute-start | bytes 1966088 | tf_op jit(solution)/shard_map/ppermute | solution.py:91
  130.1 12.9 %copy-start.4 = (bf16[160,2048]{1,0:T(8,128)(2,1)}, bf16[160,2048]{1,0:T(8,128)(2,1)S(1)}, u32[]{:S(2)}) copy-start(bf16[160,2048]{1,0:T(8,128)(2,1)S(1)} %collective-permute-done.2) | copy-start | bytes 1966084
  143.0 0.9 copy-start.5
  170.7 9.8 %copy-start.7 = (bf16[2,160,8192]{2,1,0:T(8,128)(2,1)S(1)}, bf16[2,160,8192]{2,1,0:T(8,128)(2,1)}, u32[]{:S(2)}) copy-start(bf16[2,160,8192]{2,1,0:T(8,128)(2,1)} %all-gather.4.cloned.1.call-done) | copy-start | bytes 15728644
  180.5 14.6 %copy-start.6 = (f32[128,2]{0,1:T(2,128)S(1)}, f32[128,2]{0,1:T(2,128)}, u32[]{:S(2)}) copy-start(f32[128,2]{0,1:T(2,128)} %param.8) | copy-start | bytes 3076
  180.5 30.2 %copy-start.1 = (bf16[128,768]{1,0:T(8,128)(2,1)S(1)}, bf16[128,768]{1,0:T(8,128)(2,1)}, u32[]{:S(2)}) copy-start(bf16[128,768]{1,0:T(8,128)(2,1)} %param.6) | copy-start | bytes 589828
  190.2 19.1 %all-to-all-start.2 = ((bf16[4,2,40,768]{3,2,1,0:T(8,128)(2,1)}), bf16[4,2,40,768]{3,2,1,0:T(8,128)(2,1)S(1)}, u32[]{:S(2)}, u32[]{:S(2)}) async-start(bf16[4,2,40,768]{3,2,1,0:T(8,128)(2,1)} %pad_maximum_fusion.1), calls=%async_computation.2 | async-start | bytes 983040 | tf_op jit(solution)/shard_map/all_to_all | solution.py:129
Sparse Core Ops, SparseCore 0:
  34.9 33.3 all-gather.5
  155.4 15.1 all-gather.3
